TPU v7x, 32 devices: a whole 2x2x4 slice. The times are simulated.
32 devices in a mesh: dp: 8 (over z, x), seq: 4 (over y, core).
Axes of the slice: x: 2, y: 2, z: 4, core: 2. Of those that a mesh axis runs over, the one named last changes fastest.
Arguments:
- layer_input: bfloat16 [16384, 768], P(('dp', 'seq')), may hold values from -6 to 6
- query_weight: bfloat16 [768, 768], replicated, may hold values from -0.3125 to 0.3125
- query_bias: float32 [768], replicated, may hold values from -3 to 3
- key_weight: bfloat16 [768, 768], replicated, may hold values from -0.3125 to 0.3125
- value_weight: bfloat16 [768, 768], replicated, may hold values from -0.21875 to 0.21875
- value_bias: float32 [768], replicated, may hold values from -3 to 3
- output_weight: bfloat16 [768, 768], replicated, may hold values from -1.25 to 1.25
- output_bias: float32 [768], replicated, may hold values from -1.75 to 1.75
- first_gain: float32 [768], replicated, may hold values from 0.25 to 1.75
- first_shift: float32 [768], replicated, may hold values from -1.75 to 1.75
- up_weight: bfloat16 [768, 3072], replicated, may hold values from -0.21875 to 0.21875
- up_bias: float32 [3072], replicated, may hold values from -3 to 3
- down_weight: bfloat16 [3072, 768], replicated, may hold values from -0.109375 to 0.109375
- down_bias: float32 [768], replicated, may hold values from -1.75 to 1.75
- second_gain: float32 [768], replicated, may hold values from 0.25 to 1.75
- second_shift: float32 [768], replicated, may hold values from -1.75 to 1.75
- out_cotangent: bfloat16 [16384, 768], P(('dp', 'seq')), may hold values from -6 to 6
- passage_lengths: int32 [8, 8], P('dp'), may hold values from 1 to 512, 2048 in all within a row
Outputs:
- layer_output: bfloat16 [16384, 768], P(('dp', 'seq'))
- input_grad: bfloat16 [16384, 768], P(('dp', 'seq'))
- query_weight_grad: float32 [768, 768], P(('dp', 'seq'))
- query_bias_grad: float32 [768], P(('dp', 'seq'))
- key_weight_grad: float32 [768, 768], P(('dp', 'seq'))
- value_weight_grad: float32 [768, 768], P(('dp', 'seq'))
- value_bias_grad: float32 [768], P(('dp', 'seq'))
- output_weight_grad: float32 [768, 768], P(('dp', 'seq'))
- output_bias_grad: float32 [768], P(('dp', 'seq'))
- first_gain_grad: float32 [768], P(('dp', 'seq'))
- first_shift_grad: float32 [768], P(('dp', 'seq'))
- up_weight_grad: float32 [768, 3072], P(('dp', 'seq'))
- up_bias_grad: float32 [3072], P(('dp', 'seq'))
- down_weight_grad: float32 [3072, 768], P(('dp', 'seq'))
- down_bias_grad: float32 [768], P(('dp', 'seq'))
- second_gain_grad: float32 [768], P(('dp', 'seq'))
- second_shift_grad: float32 [768], P(('dp', 'seq'))
Inputs may be any that keep to these rules, and one draw needn't show every extreme that they name: `passage_lengths`: each row lists the passages of one group in order; a row sums to 2048 and its longest passage has exactly 512 tokens.
All inputs are finite; a program needn't handle non-finite values.
Results may differ from a plain program's by a relative error of at most 0.015.
The roundings to bfloat16 on the way count: a program that leaves them out, or rounds other values in their place, can miss the bound.
Values may be sent and summed in bfloat16 or wider, within the bound.
A program may use at most 192 MiB of HBM per device.

v0:
```python
import functools

import jax
import jax.numpy as jnp
from jax import lax
from jax.experimental import pallas as pl
from jax.experimental.pallas import tpu as pltpu
from jax.sharding import PartitionSpec as P

HEAD_DIM = 64
PAIR = 2 * HEAD_DIM
AXES = ("dp", "seq")
NEG = -1e30
FLOOR = -3e38
BQ = 256
BK = 128
LEVELS = 5
layer_eps = 1e-12
F32 = jnp.float32
BF16 = jnp.bfloat16


def nn(a, b):
    return lax.dot_general(a, b, (((1,), (0,)), ((), ())), preferred_element_type=F32)


def nt(a, b):
    return lax.dot_general(a, b, (((1,), (1,)), ((), ())), preferred_element_type=F32)


def tn(a, b):
    return lax.dot_general(a, b, (((0,), (0,)), ((), ())), preferred_element_type=F32)


def cost(flops, nbytes, trans=0):
    return pl.CostEstimate(flops=int(flops), bytes_accessed=int(nbytes), transcendentals=int(trans))


def params(limit=56 << 20):
    return pltpu.CompilerParams(vmem_limit_bytes=limit)


def whole():
    return pl.BlockSpec(memory_space=pltpu.VMEM)


def hbm():
    return pl.BlockSpec(memory_space=pl.ANY)


def low_lanes():
    return lax.broadcasted_iota(jnp.int32, (1, PAIR), 1) < HEAD_DIM


def line(ref):
    return ref[...].reshape(1, -1)


def remote_params(number):
    return pltpu.CompilerParams(
        vmem_limit_bytes=60 << 20, collective_id=number, has_side_effects=True
    )


class Links:
    def __init__(self, ndev, parts, send_sems, recv_sems):
        self.ndev, self.parts = ndev, parts
        self.place = lax.axis_index("seq")
        self.row = lax.axis_index("dp")
        self.me = self.row * parts + self.place
        self.shift = ndev >> LEVELS
        self.block = self.me // self.shift
        self.send_sems, self.recv_sems = send_sems, recv_sems
        self.used = 0
        self.started = []
        self.has_prev = self.place > 0
        self.has_next = self.place < parts - 1

    def partner(self, *flips):
        other = self.me
        for flip in flips:
            other = other + (1 - 2 * ((self.me // flip) % 2)) * flip
        return (other // self.parts, other % self.parts)

    def greet(self, flips, neighbours):
        barrier = pltpu.get_barrier_semaphore()

        def signal(device):
            pl.semaphore_signal(
                barrier, inc=1, device_id=device, device_id_type=pl.DeviceIdType.MESH
            )

        for flip in flips:
            signal(self.partner(*(flip if isinstance(flip, tuple) else (flip,))))
        if neighbours:

            @pl.when(self.has_prev)
            def _():
                signal((self.row, self.place - 1))

            @pl.when(self.has_next)
            def _():
                signal((self.row, self.place + 1))

        count = len(flips)
        if neighbours:
            count = count + jnp.minimum(self.place, 1)
            count = count + jnp.minimum(self.parts - 1 - self.place, 1)
        pl.semaphore_wait(barrier, count)

    def make(self, src, dst, device):
        n = self.used
        self.used += 1
        return pltpu.make_async_remote_copy(
            src_ref=src, dst_ref=dst, send_sem=self.send_sems.at[n],
            recv_sem=self.recv_sems.at[n], device_id=device,
            device_id_type=pl.DeviceIdType.MESH,
        )

    def exchange(self, src, dst, *flips):
        copy = self.make(src, dst, self.partner(*flips))
        copy.start()
        self.started.append(copy)
        return copy

    def finish(self):
        for copy in self.started:
            copy.wait_send()

    def neighbours(self, src, at_next, at_prev):
        ahead = self.make(src, at_next, (self.row, self.place + 1))
        back = self.make(src, at_prev, (self.row, self.place - 1))

        @pl.when(self.has_next)
        def _():
            ahead.start()

        @pl.when(self.has_prev)
        def _():
            back.start()

        return ahead, back

    def from_prev(self, pair):
        @pl.when(self.has_prev)
        def _():
            pair[0].wait_recv()

    def from_next(self, pair):
        @pl.when(self.has_next)
        def _():
            pair[1].wait_recv()

    def sent(self, pair):
        @pl.when(self.has_next)
        def _():
            pair[0].wait_send()

        @pl.when(self.has_prev)
        def _():
            pair[1].wait_send()


def both(a, b):
    return (a.astype(F32) + b.astype(F32)).astype(BF16)


class Chain:
    def __init__(self, links, buf, recv, order, step):
        self.links, self.buf, self.recv, self.order, self.step = links, buf, recv, order, step
        self.base = 0

    def position(self, c):
        at = 0
        for k, b in enumerate(self.order):
            mine, its = (self.links.block // (1 << b)) % 2, (c // (1 << b)) % 2
            at = at + (mine + its - 2 * mine * its) * (1 << (LEVELS - 1 - k))
        return at

    def send(self):
        self.half = (1 << LEVELS) >> (self.step + 1)
        self.copy = self.links.exchange(
            self.buf.at[pl.ds(self.half, self.half)],
            self.recv.at[pl.ds(self.base, self.half)],
            self.links.shift << self.order[self.step],
        )

    def receive(self):
        self.copy.wait_recv()
        self.base += self.half
        self.step += 1

    def add(self):
        base, half, buf, recv = self.base, self.half, self.buf, self.recv
        self.receive()
        if half > 1:

            @pl.loop(0, half)
            def _(i):
                buf[i] = both(buf[i], recv[base + i])

            self.send()

    def last(self):
        return self.buf[0].astype(F32) + self.recv[self.base - 1].astype(F32)


class Flat:
    def __init__(self, links, buf, recvs, bits, order, step, cols=None):
        self.links, self.buf, self.recvs = links, buf, list(recvs)
        self.bits, self.order, self.step = bits, order, step
        self.at = [slice(None)] * len(bits)
        self.rows = buf.shape[len(bits)]
        self.cols = slice(None) if cols is None else cols

    def view(self, lead, start, size):
        index = tuple(i if isinstance(i, int) else slice(None) for i in lead)
        return self.buf.at[index + (pl.ds(start, size), self.cols)]

    def send(self):
        bit = self.order[self.step]
        shift = self.links.shift
        self.recv = self.recvs.pop(0)
        if isinstance(bit, tuple):
            self.rows //= 4
            self.copies = [
                self.links.exchange(
                    self.view(self.at, n * self.rows, self.rows),
                    self.recv.at[n - 1],
                    *(shift << b for k, b in enumerate(bit) if (n >> (1 - k)) & 1),
                )
                for n in (1, 2, 3)
            ]
            return
        if bit in self.bits:
            lead = list(self.at)
            lead[self.bits.index(bit)] = 1
            src = self.view(lead, 0, self.rows)
            self.at[self.bits.index(bit)] = 0
        else:
            self.rows //= 2
            src = self.view(self.at, self.rows, self.rows)
        self.copies = [self.links.exchange(src, self.recv, shift << bit)]

    def add(self):
        for copy in self.copies:
            copy.wait_recv()
        self.step += 1
        if self.step == len(self.order):
            return
        leads = [()]
        for i in self.at:
            leads = [a + (b,) for a in leads for b in ((0, 1) if i != 0 else (0,))]
        free = [n for n, i in enumerate(self.at) if i != 0]
        buf, recv, cols = self.buf, self.recv, self.cols

        @pl.loop(0, self.rows // 16)
        def _(i):
            at = pl.ds(pl.multiple_of(i * 16, 16), 16)
            for lead in leads:
                from_ = tuple(lead[n] for n in free)
                to = lead + (at, cols)
                buf[to] = both(buf[to], recv[from_ + (at,)])

        self.send()

    def last(self):
        lead = (0,) * len(self.bits)
        total = self.buf[lead + (slice(0, self.rows), self.cols)].astype(F32)
        if isinstance(self.order[-1], tuple):
            for n in range(3):
                total = total + self.recv[n].astype(F32)
            return total
        return total + self.recv[...].astype(F32)


def flat_recvs(bits, order, step, cols, blocks_rows):
    lead, rows = len(bits), blocks_rows
    shapes = []
    for bit in order[step:]:
        if isinstance(bit, tuple):
            shapes.append((3, rows // 4, cols))
            continue
        if bit in bits:
            lead -= 1
        else:
            rows //= 2
        shapes.append((2,) * lead + (rows, cols))
    return shapes


def shuffle(links, width):
    short = width // BLOCKS
    col = lax.broadcasted_iota(jnp.int32, (8, width), 1)
    source = col
    for p in range(BLOCKS):
        c = 0
        for k, b in enumerate(FLAT):
            mine, its = (links.block // (1 << b)) % 2, (p >> (LEVELS - 1 - k)) & 1
            c = c + (mine + its - 2 * mine * its) * (1 << b)
        source = jnp.where(col >= p * short, col + (c - p) * short, source)
    row = lax.broadcasted_iota(jnp.int32, (width, width), 0)
    return (row == source[0:1]).astype(F32).astype(BF16)


FLAT = (0, 2, 1, 3, 4)
DN_ONE = (0, 2, 1, 3, 4)
DN_TWO = (0, 1, 2, 3, 4)
UP_ONE = (0, 2, 1, 3, 4)
UP_TWO = (0, 3, 2, 1, 4)
OUT_ORDER = (0, 2, 1, 3, 4)
LEFT_ORDER = (0, 2, 1, (3, 4))
RIGHT_ORDER = (0, 1, 2, (3, 4))
BLOCKS = 1 << LEVELS


def first_kernel(
    ndev, parts, x_ref, lengths, wq_hbm, bq, wk_hbm, wv_hbm, bv,
    q_hbm, k_hbm, v_hbm, onehot, qmask, bounds, mix, xp,
    halo, wq, wk, wv, q_ref, k_ref, v_ref, load_sems, store_sems, send_sems, recv_sems,
):
    rows, width = x_ref.shape
    count = rows * parts
    loads = [
        pltpu.make_async_copy(src, dst, load_sems.at[n])
        for n, (src, dst) in enumerate(((wq_hbm, wq), (wk_hbm, wk), (wv_hbm, wv)))
    ]
    for load in loads:
        load.start()
    links = Links(ndev, parts, send_sems, recv_sems)
    links.greet([], True)
    step = rows // 2
    pairs = [
        links.neighbours(
            x_ref.at[pl.ds(h * step, step)],
            halo.at[pl.ds(h * step, step)],
            halo.at[pl.ds(2 * rows + h * step, step)],
        )
        for h in range(2)
    ]

    @pl.when(jnp.logical_not(links.has_prev))
    def _():
        halo[0:rows, :] = jnp.zeros((rows, width), BF16)

    @pl.when(jnp.logical_not(links.has_next))
    def _():
        halo[2 * rows : 3 * rows, :] = jnp.zeros((rows, width), BF16)

    halo[rows : 2 * rows, :] = x_ref[...]

    for load in loads:
        load.wait()

    def stores(at, n):
        part = pl.ds(at, step)
        return [
            pltpu.make_async_copy(src.at[part], dst.at[part], store_sems.at[n, m])
            for m, (src, dst) in enumerate(((q_ref, q_hbm), (k_ref, k_hbm), (v_ref, v_hbm)))
        ]

    def chunk(t):
        return jnp.where(t < 2, 2 + t, (t % 2) * 4 + t // 2 - 1)

    def project(t):
        at = pl.multiple_of(chunk(t) * step, step)
        rows_at = pl.ds(at, step)
        x = halo[rows_at, :]
        q_ref[rows_at, :] = (nn(x, wq[...]) + line(bq)).astype(BF16)
        k_ref[rows_at, :] = nn(x, wk[...]).astype(BF16)
        v_ref[rows_at, :] = (nn(x, wv[...]) + line(bv)).astype(BF16)
        for copy in stores(at, t):
            copy.start()

    pl.loop(0, 2)(project)

    slots = lengths.shape[1]
    ends, total = [], jnp.int32(0)
    for n in range(slots):
        total = total + lengths[0, n]
        ends.append(total)
    start = (links.place - 1) * rows
    lane = lax.broadcasted_iota(jnp.int32, (BQ, PAIR), 1) % HEAD_DIM
    one, none, far = BF16(1.0), BF16(0.0), BF16(NEG)

    @pl.loop(0, 3 * rows // BQ)
    def _(i):
        at = start + i * BQ
        where = at + lax.broadcasted_iota(jnp.int32, (BQ, PAIR), 0)
        seg = jnp.zeros((BQ, PAIR), jnp.int32)
        for end in ends:
            seg = seg + (where >= end).astype(jnp.int32)
        outside = (where < 0) | (where >= count)
        seg = jnp.where(outside, slots, seg)
        match = (seg == lane).astype(F32)
        to = pl.ds(pl.multiple_of(i * BQ, BQ), BQ)
        onehot[to, :] = match.astype(BF16)
        qmask[to, :] = ((1.0 - match) * NEG).astype(BF16)

    mix[...] = shuffle(links, width)
    xp[...] = nn(x_ref[...], mix[...]).astype(BF16)

    for n in range(rows // BQ):
        near = links.place * rows + n * BQ
        far_row = near + BQ - 1
        lo, hi = jnp.int32(0), jnp.int32(count)
        for end in ends:
            lo = jnp.where(end <= near, jnp.maximum(lo, end), lo)
            hi = jnp.where(end > far_row, jnp.minimum(hi, end), hi)
        lo = jnp.maximum(lo - start, 0)
        hi = jnp.minimum(hi - start, 3 * rows)
        bounds[0, n] = lo // BK
        bounds[1, n] = (hi + BK - 1) // BK

    @pl.loop(2, 6)
    def _(t):
        for h in range(2):

            @pl.when(t == 2 + 2 * h)
            def _():
                links.from_prev(pairs[h])

            @pl.when(t == 3 + 2 * h)
            def _():
                links.from_next(pairs[h])

        project(t)

    for pair in pairs:
        links.sent(pair)

    @pl.loop(0, 6)
    def _(t):
        for copy in stores(pl.multiple_of(chunk(t) * step, step), t):
            copy.wait()


def first(ndev, parts, x, lengths, wq, bq, wk, wv, bv):
    rows, width = x.shape
    ext = jax.ShapeDtypeStruct((3 * rows, width), BF16)
    seg = jax.ShapeDtypeStruct((3 * rows, PAIR), BF16)
    smem = pl.BlockSpec(memory_space=pltpu.SMEM)
    return pl.pallas_call(
        functools.partial(first_kernel, ndev, parts),
        in_specs=[whole(), smem, hbm(), whole(), hbm(), hbm(), whole()],
        out_specs=[hbm()] * 3 + [whole()] * 2 + [smem] + [whole()] * 2,
        out_shape=[ext] * 3
        + [seg] * 2
        + [
            jax.ShapeDtypeStruct((2, rows // BQ), jnp.int32),
            jax.ShapeDtypeStruct((width, width), BF16),
            jax.ShapeDtypeStruct((rows, width), BF16),
        ],
        scratch_shapes=[
            pltpu.VMEM((3 * rows, width), BF16),
            pltpu.VMEM((width, width), BF16),
            pltpu.VMEM((width, width), BF16),
            pltpu.VMEM((width, width), BF16),
            pltpu.VMEM((3 * rows, width), BF16),
            pltpu.VMEM((3 * rows, width), BF16),
            pltpu.VMEM((3 * rows, width), BF16),
            pltpu.SemaphoreType.DMA((3,)),
            pltpu.SemaphoreType.DMA((6, 3)),
            pltpu.SemaphoreType.DMA((4,)),
            pltpu.SemaphoreType.DMA((4,)),
        ],
        compiler_params=remote_params(0),
        cost_estimate=cost(15e9, 12 << 20),
        name="first",
    )(x, lengths, wq, bq, wk, wv, bv)


def lengths_of(rows):
    most = BQ // BK + 2 * -(-(rows - 1) // BK)
    return [n for n in range(3, most) if n <= 6 or n % 2 == 0] + [most]


def key_range(bounds, i, rows):
    lo, hi = bounds[0, i], bounds[1, i]
    sizes = lengths_of(rows)
    number = jnp.int32(sizes[-1])
    for n in reversed(sizes):
        number = jnp.where(hi - lo <= n, n, number)
    return jnp.minimum(lo, 3 * rows // BK - number), number


def forward_kernel(bounds, q_ref, k_ref, v_ref, onehot, qmask, ctx_ref, lse_ref, ka, kb):
    rows = ctx_ref.shape[0]
    low = low_lanes()
    key, hot = k_ref[...], onehot[...]
    ka[...] = jnp.where(low, key, hot)
    kb[...] = jnp.where(low, hot, key)

    @pl.loop(0, rows // BQ)
    def _(i):
        first_block, number = key_range(bounds, i, rows)
        base = pl.multiple_of(first_block * BK, BK)
        at = pl.ds(pl.multiple_of(i * BQ, BQ), BQ)
        own = pl.ds(pl.multiple_of(rows + i * BQ, BQ), BQ)
        for num in lengths_of(rows):

            @pl.when(number == num)
            def _():
                span = pl.ds(base, num * BK)
                query = q_ref[own, :] * BF16(HEAD_DIM**-0.5)
                mask = qmask[own, :]
                parts = []
                for head, keys in enumerate((ka, kb)):
                    pick = (query, mask) if head == 0 else (mask, query)
                    scores = nt(jnp.where(low, *pick), keys[span, :])
                    top = jnp.max(scores, axis=1, keepdims=True)
                    weights = jnp.exp(scores - top)
                    total = jnp.sum(weights, axis=1, keepdims=True)
                    acc = nn(weights.astype(BF16), v_ref[span, :])
                    parts.append((acc / total, top + jnp.log(total)))
                ctx_ref[at, :] = jnp.where(low, parts[0][0], parts[1][0])
                flip = jnp.where(low, parts[0][1], parts[1][1]).T
                lse_ref[0, 0:1, at] = flip[0:1]
                lse_ref[0, 1:2, at] = flip[HEAD_DIM : HEAD_DIM + 1]


def attend_forward(bounds, q, k, v, onehot, qmask):
    rows, width = q.shape[0] // 3, q.shape[1]
    pairs = width // PAIR
    ext = pl.BlockSpec((3 * rows, PAIR), lambda p, *_: (0, p))
    seg = pl.BlockSpec((3 * rows, PAIR), lambda p, *_: (0, 0))
    grid = pltpu.PrefetchScalarGridSpec(
        num_scalar_prefetch=1,
        grid=(pairs,),
        in_specs=[ext, ext, ext, seg, seg],
        out_specs=[
            pl.BlockSpec((rows, PAIR), lambda p, *_: (0, p)),
            pl.BlockSpec((1, 2, rows), lambda p, *_: (p, 0, 0)),
        ],
        scratch_shapes=[pltpu.VMEM((3 * rows, PAIR), BF16)] * 2,
    )
    return pl.pallas_call(
        forward_kernel,
        grid_spec=grid,
        out_shape=[
            jax.ShapeDtypeStruct((rows, width), F32),
            jax.ShapeDtypeStruct((pairs, 2, rows), F32),
        ],
        compiler_params=params(),
        cost_estimate=cost(20e9, 24 * rows * width),
        name="attend_forward",
    )(bounds, q, k, v, onehot, qmask)


def backward_kernel(
    bounds, q_ref, k_ref, v_ref, g_ref, stat_ref, onehot, qmask,
    dq_ref, dk_ref, dv_ref, ka, kb, qa, qb, qs,
):
    rows = dq_ref.shape[0]
    low = low_lanes()
    zero = jnp.zeros((1, PAIR), BF16)
    scale = BF16(HEAD_DIM**-0.5)
    key, hot = k_ref[...], onehot[...]
    ka[...] = jnp.where(low, key, hot)
    kb[...] = jnp.where(low, hot, key)
    query, mask = q_ref[...] * scale, qmask[...]
    qa[...] = jnp.where(low, query, mask)
    qb[...] = jnp.where(low, mask, query)
    qs[...] = query

    @pl.loop(0, rows // BQ)
    def _(i):
        first_block, number = key_range(bounds, i, rows)
        base = pl.multiple_of(first_block * BK, BK)
        at = pl.ds(pl.multiple_of(i * BQ, BQ), BQ)
        own = pl.ds(pl.multiple_of(rows + i * BQ, BQ), BQ)
        for num in lengths_of(rows):

            @pl.when(number == num)
            def _():
                span = pl.ds(base, num * BK)

                def pick(head, value, other):
                    return jnp.where(low, value, other) if head == 0 else jnp.where(
                        low, other, value
                    )

                columns = stat_ref[0, :, own]
                columns = jnp.concatenate([columns, columns], axis=0).T
                out = []
                for head, keys in enumerate((ka, kb)):
                    queries = (qa, qb)[head][own, :]
                    grads = pick(head, g_ref[own, :], zero)
                    scores = nt(queries, keys[span, :])
                    prob_grad = nt(grads, v_ref[span, :])
                    probs = jnp.exp(scores - columns[:, head : head + 1])
                    delta = columns[:, 2 + head : 3 + head]
                    score_grad = (probs * (prob_grad - delta)).astype(BF16)
                    out.append(nn(score_grad, k_ref[span, :]))
                dq = jnp.where(low, out[0], out[1]) * F32(HEAD_DIM**-0.5)
                dq_ref[at, :] = dq.astype(BF16)
                out = []
                for head, queries in enumerate((qa, qb)):
                    keys = (ka, kb)[head][own, :]
                    vals = pick(head, v_ref[own, :], zero)
                    scores = nt(keys, queries[span, :])
                    prob_grad = nt(vals, g_ref[span, :])
                    probs = jnp.exp(scores - stat_ref[0, head : head + 1, span])
                    delta = stat_ref[0, 2 + head : 3 + head, span]
                    score_grad = (probs * (prob_grad - delta)).astype(BF16)
                    out.append((
                        nn(score_grad, qs[span, :]),
                        nn(probs.astype(BF16), g_ref[span, :]),
                    ))
                dk_ref[at, :] = jnp.where(low, out[0][0], out[1][0]).astype(BF16)
                dv_ref[at, :] = jnp.where(low, out[0][1], out[1][1]).astype(BF16)


def attend_backward(bounds, q, k, v, g, stat, onehot, qmask):
    rows, width = q.shape[0] // 3, q.shape[1]
    pairs = width // PAIR
    ext = pl.BlockSpec((3 * rows, PAIR), lambda p, *_: (0, p))
    own = pl.BlockSpec((rows, PAIR), lambda p, *_: (0, p))
    seg = pl.BlockSpec((3 * rows, PAIR), lambda p, *_: (0, 0))
    grid = pltpu.PrefetchScalarGridSpec(
        num_scalar_prefetch=1,
        grid=(pairs,),
        in_specs=[ext] * 4 + [pl.BlockSpec((1, 4, 3 * rows), lambda p, *_: (p, 0, 0)), seg, seg],
        out_specs=[own] * 3,
        scratch_shapes=[pltpu.VMEM((3 * rows, PAIR), BF16)] * 5,
    )
    return pl.pallas_call(
        backward_kernel,
        grid_spec=grid,
        out_shape=[jax.ShapeDtypeStruct((rows, width), BF16)] * 3,
        compiler_params=params(),
        cost_estimate=cost(40e9, 40 * rows * width),
        name="attend_backward",
    )(bounds, q, k, v, g, stat, onehot, qmask)


def norm_forward(h):
    mean = jnp.mean(h, axis=-1, keepdims=True)
    centred = h - mean
    variance = jnp.mean(centred * centred, axis=-1, keepdims=True)
    inverse = lax.rsqrt(variance + layer_eps)
    return centred * inverse, inverse


def norm_backward(grad, gain, hat, inverse):
    g = grad * gain
    return inverse * (
        g - jnp.mean(g, axis=-1, keepdims=True) - hat * jnp.mean(g * hat, axis=-1, keepdims=True)
    )


def colsum(v):
    return jnp.sum(v, axis=0, keepdims=True)


def middle_kernel(
    ndev, parts,
    x_ref, ctx_ref, ct_ref, wo, bo, g1, s1, wup_hbm, bup, wdn_hbm, bdn, g2, s2, lse_ref, mix,
    result_hbm, fg_hbm, g_hbm, stat_ref, vec_ref, bup_ref,
    one_keep_hbm, one_send_hbm, two_keep_hbm, two_send_hbm, upa_keep_hbm, upa_send_hbm, upb_keep_hbm,
    upb_send_hbm, wo_keep_hbm, wo_send_hbm,
    wup, wdn, hid, nl, nlp, bg, cl, ag, slope, normed, inv, acc, grad_s,
    result_ref, fg_ref, g_ref,
    one_s, one_r, two_s, two_r, up_s, up_r, wo_s, wo_r,
    load_sems, store_sems, send_sems, recv_sems,
):
    stores = []

    def store(src, dst):
        copy = pltpu.make_async_copy(src, dst, store_sems.at[len(stores)])
        copy.start()
        stores.append(copy)

    rows, width = x_ref.shape
    ff = wup.shape[1]
    rc, fc = 256, 1024
    chunks, tiles = rows // rc, ff // fc
    tall, short = ff // BLOCKS, width // BLOCKS
    up_copy = pltpu.make_async_copy(wup_hbm, wup, load_sems.at[0])
    dn_copy = pltpu.make_async_copy(wdn_hbm, wdn, load_sems.at[1])
    up_copy.start()
    dn_copy.start()
    links = Links(ndev, parts, send_sems, recv_sems)
    links.greet([links.shift << DN_ONE[0], links.shift << DN_ONE[1]], True)
    one = Chain(links, one_s, one_r, DN_ONE, 0)
    two = Chain(links, two_s, two_r, DN_TWO, 0)
    @pl.loop(0, chunks)
    def _(r):
        at = pl.ds(pl.multiple_of(r * rc, rc), rc)
        c_low = ctx_ref[at, :].astype(BF16)
        cl[at, :] = nn(c_low, mix[...]).astype(BF16)
        h = x_ref[at, :].astype(F32) + (nn(c_low, wo[...]) + line(bo))
        xhat, inverse = norm_forward(h)
        res = xhat * line(g1) + line(s1)
        fg_ref[at, :] = xhat
        inv[at, :] = inverse
        normed[at, :] = res
        low = res.astype(BF16)
        nl[at, :] = low
        nlp[at, :] = nn(low, mix[...]).astype(BF16)

    up_copy.wait()
    dn_copy.wait()
    acc[...] = jnp.zeros_like(acc)

    @pl.loop(0, tiles)
    def _(j):
        cols = pl.ds(pl.multiple_of(j * fc, fc), fc)
        bias = bup[cols].reshape(1, fc)

        @pl.loop(0, chunks)
        def _(r):
            at = pl.ds(pl.multiple_of(r * rc, rc), rc)
            up = nn(nl[at, :], wup[:, cols]) + bias
            cdf = 0.5 * (1.0 + lax.erf(up * F32(0.5**0.5)))
            density = jnp.exp(-0.5 * up * up) * F32(0.3989422804014327)
            slope[at, cols] = cdf + up * density
            act = (up * cdf).astype(BF16)
            hid[at, cols] = act
            acc[at, :] = acc[at, :] + nn(act, wdn[cols, :])

    vec_ref[...] = jnp.zeros_like(vec_ref)

    @pl.loop(0, chunks)
    def _(r):
        at = pl.ds(pl.multiple_of(r * rc, rc), rc)
        xhat, inverse = norm_forward(normed[at, :] + (acc[at, :] + line(bdn)))
        result_ref[at, :] = (xhat * line(g2) + line(s2)).astype(BF16)
        ct = ct_ref[at, :].astype(F32)
        second = norm_backward(ct, line(g2), xhat, inverse)
        low = second.astype(BF16)
        bg[at, :] = low
        acc[at, :] = second
        vec_ref[0:1, :] = vec_ref[0:1, :] + colsum(ct * xhat)
        vec_ref[1:2, :] = vec_ref[1:2, :] + colsum(ct)
        vec_ref[2:3, :] = vec_ref[2:3, :] + colsum(low.astype(F32))

    store(result_ref, result_hbm)

    some = width // tall

    @pl.loop(0, ff // width)
    def _(j):
        grad_s[...] = tn(hid[:, pl.ds(pl.multiple_of(j * width, width), width)], bg[...])

        @pl.loop(0, some)
        def _(c):
            base = pl.multiple_of(c * tall, tall // 2)
            one_s[one.position(j * some + c)] = grad_s[pl.ds(base, tall // 2), :].astype(BF16)
            base = pl.multiple_of(c * tall + tall // 2, tall // 2)
            two_s[two.position(j * some + c)] = grad_s[pl.ds(base, tall // 2), :].astype(BF16)

    one.send()
    two.send()

    def back_tiles(lo, hi):
        @pl.loop(lo, hi)
        def _(j):
            cols = pl.ds(pl.multiple_of(j * fc, fc), fc)
            bup_ref[:, cols] = jnp.zeros((1, fc), F32)

            @pl.loop(0, chunks)
            def _(r):
                at = pl.ds(pl.multiple_of(r * rc, rc), rc)
                grad = (nt(bg[at, :], wdn[cols, :]) * slope[at, cols]).astype(BF16)
                hid[at, cols] = grad
                bup_ref[:, cols] = bup_ref[:, cols] + colsum(grad.astype(F32))
                acc[at, :] = acc[at, :] + nt(grad, wup[:, cols])

    back_tiles(0, tiles - 1)
    one.add()
    back_tiles(tiles - 1, tiles)

    zero_prev = pltpu.make_async_copy(
        result_ref, g_hbm.at[pl.ds(0, rows)], store_sems.at[store_sems.shape[0] - 2]
    )
    zero_next = pltpu.make_async_copy(
        result_ref, g_hbm.at[pl.ds(2 * rows, rows)], store_sems.at[store_sems.shape[0] - 1]
    )
    stores.pop().wait()
    result_ref[...] = jnp.zeros_like(result_ref)

    @pl.when(jnp.logical_not(links.has_prev))
    def _():
        zero_prev.start()
        stat_ref[:, :, 0:rows] = jnp.zeros((width // PAIR, 4, rows), F32)

    @pl.when(jnp.logical_not(links.has_next))
    def _():
        zero_next.start()
        stat_ref[:, :, 2 * rows : 3 * rows] = jnp.zeros((width // PAIR, 4, rows), F32)

    pairs = []
    for r in range(chunks):
        at = slice(r * rc, (r + 1) * rc)
        mid = slice(rows + r * rc, rows + (r + 1) * rc)
        total = acc[at, :]
        xhat = fg_ref[at, :]
        first_grad = norm_backward(total, line(g1), xhat, inv[at, :])
        fg_ref[at, :] = first_grad
        low = first_grad.astype(BF16)
        ag[at, :] = low
        vec_ref[3:4, :] = vec_ref[3:4, :] + colsum(total * xhat)
        vec_ref[4:5, :] = vec_ref[4:5, :] + colsum(total)
        vec_ref[5:6, :] = vec_ref[5:6, :] + colsum(low.astype(F32))
        cg = nt(low, wo[...]).astype(BF16)
        g_ref[at, :] = cg
        pairs.append(links.neighbours(
            g_ref.at[pl.ds(r * rc, rc)],
            g_hbm.at[pl.ds(r * rc, rc)],
            g_hbm.at[pl.ds(2 * rows + r * rc, rc)],
        ))
        prod = cg.astype(F32) * ctx_ref[at, :]
        for p in range(width // PAIR):
            flip = prod[:, p * PAIR : (p + 1) * PAIR].T
            stat_ref[p, 2:3, mid] = colsum(flip[:HEAD_DIM])
            stat_ref[p, 3:4, mid] = colsum(flip[HEAD_DIM:])
    store(g_ref, g_hbm.at[pl.ds(rows, rows)])
    store(fg_ref, fg_hbm)
    for p in range(width // PAIR):
        stat_ref[p, 0:2, rows : 2 * rows] = lse_ref[p]
    pairs.append(links.neighbours(
        stat_ref.at[:, :, pl.ds(rows, rows)],
        stat_ref.at[:, :, pl.ds(0, rows)],
        stat_ref.at[:, :, pl.ds(2 * rows, rows)],
    ))

    quarter = width // 8
    ups = []
    for n in range(2):

        @pl.loop(0, 2)
        def _(t):
            cols = pl.ds(pl.multiple_of(n * (ff // 2) + t * width, width), width)
            grad = tn(nlp[...], hid[:, cols])
            up_s[:, :, :, :, cols] = grad.astype(BF16).reshape(2, 2, 2, quarter, width)

        cols = pl.ds(n * (ff // 2), ff // 2)
        ups.append(links.exchange(
            up_s.at[1, :, :, :, cols], up_r.at[:, :, :, cols], links.shift << FLAT[0]
        ))

    wo_s[...] = tn(cl[...], ag[...]).astype(BF16).reshape(2, 2, 2, quarter, width)
    out = links.exchange(wo_s.at[1], wo_r, links.shift << FLAT[0])

    def settle(chain, keep, send):
        chain.receive()
        half, quarter = BLOCKS // 2, BLOCKS // 4

        @pl.loop(0, half)
        def _(i):
            chain.recv[i] = both(chain.buf[i], chain.recv[i])

        store(chain.recv.at[pl.ds(0, quarter)], keep)
        store(chain.recv.at[pl.ds(quarter, quarter)], send)

    settle(two, two_keep_hbm, two_send_hbm)

    def settle_flat(copy, mine, got, cols):
        copy.wait_recv()

        @pl.loop(0, quarter // 16)
        def _(i):
            at = pl.ds(pl.multiple_of(i * 16, 16), 16)
            for x_bit in range(2):
                for y_bit in range(2):
                    index = (x_bit, y_bit, at, cols)
                    got[index] = both(mine[(0,) + index], got[index])

    left, right = pl.ds(0, ff // 2), pl.ds(ff // 2, ff // 2)
    settle_flat(ups[0], up_s, up_r, left)
    store(up_r.at[0, :, :, left], upa_keep_hbm)
    store(up_r.at[1, :, :, left], upa_send_hbm)
    settle_flat(ups[1], up_s, up_r, right)
    store(up_r.at[:, :, pl.ds(0, quarter // 2), right], upb_keep_hbm)
    store(up_r.at[:, :, pl.ds(quarter // 2, quarter // 2), right], upb_send_hbm)
    settle_flat(out, wo_s, wo_r, slice(None))
    store(wo_r.at[0], wo_keep_hbm)
    store(wo_r.at[1], wo_send_hbm)
    one.receive()

    @pl.loop(0, BLOCKS // 4)
    def _(i):
        one_s[i] = both(one_s[i], one_r[BLOCKS // 2 + i])

    store(one_s.at[pl.ds(0, BLOCKS // 8)], one_keep_hbm)
    store(one_s.at[pl.ds(BLOCKS // 8, BLOCKS // 8)], one_send_hbm)
    for copy in stores:
        copy.wait()

    @pl.when(jnp.logical_not(links.has_prev))
    def _():
        zero_prev.wait()

    @pl.when(jnp.logical_not(links.has_next))
    def _():
        zero_next.wait()

    for pair in pairs:
        links.from_prev(pair)
        links.from_next(pair)
        links.sent(pair)
    links.finish()


def middle(ndev, parts, x, ctx, ct, wo, bo, g1, s1, wup, bup, wdn, bdn, g2, s2, lse, mix):
    rows, width = x.shape
    ff = wup.shape[1]
    pairs = width // PAIR
    tall, short = ff // BLOCKS, width // BLOCKS
    left = BLOCKS // 4

    def out(*shape, dtype=BF16):
        return jax.ShapeDtypeStruct(shape, dtype)

    shapes = [
        out(rows, width),
        out(rows, width, dtype=F32),
        out(3 * rows, width),
        out(pairs, 4, 3 * rows, dtype=F32),
        out(8, width, dtype=F32),
        out(1, ff, dtype=F32),
        out(left // 2, tall // 2, width),
        out(left // 2, tall // 2, width),
        out(left, tall // 2, width),
        out(left, tall // 2, width),
        out(2, width // 8, ff // 2),
        out(2, width // 8, ff // 2),
        out(2, 2, width // 16, ff // 2),
        out(2, 2, width // 16, ff // 2),
        out(2, width // 8, width),
        out(2, width // 8, width),
    ]

    def chain(*shape):
        return [pltpu.VMEM((BLOCKS,) + shape, BF16), pltpu.VMEM((BLOCKS // 2,) + shape, BF16)]

    dn_one = chain(tall // 2, width)
    dn_one[1] = pltpu.VMEM((3 * BLOCKS // 4, tall // 2, width), BF16)
    copies = 6 + 6
    return pl.pallas_call(
        functools.partial(middle_kernel, ndev, parts),
        in_specs=[whole()] * 7 + [hbm(), whole(), hbm()] + [whole()] * 5,
        out_specs=[hbm()] * 3 + [whole()] * 3 + [hbm()] * 10,
        out_shape=shapes,
        scratch_shapes=[
            pltpu.VMEM((width, ff), BF16),
            pltpu.VMEM((ff, width), BF16),
            pltpu.VMEM((rows, ff), BF16),
            pltpu.VMEM((rows, width), BF16),
            pltpu.VMEM((rows, width), BF16),
            pltpu.VMEM((rows, width), BF16),
            pltpu.VMEM((rows, width), BF16),
            pltpu.VMEM((rows, width), BF16),
            pltpu.VMEM((rows, ff), F32),
            pltpu.VMEM((rows, width), F32),
            pltpu.VMEM((rows, 1), F32),
            pltpu.VMEM((rows, width), F32),
            pltpu.VMEM((width, width), F32),
            pltpu.VMEM((rows, width), BF16),
            pltpu.VMEM((rows, width), F32),
            pltpu.VMEM((rows, width), BF16),
        ]
        + dn_one + chain(tall // 2, width)
        + [
            pltpu.VMEM((2, 2, 2, width // 8, ff), BF16),
            pltpu.VMEM((2, 2, width // 8, ff), BF16),
            pltpu.VMEM((2, 2, 2, width // 8, width), BF16),
            pltpu.VMEM((2, 2, width // 8, width), BF16),
        ]
        + [
            pltpu.SemaphoreType.DMA((2,)),
            pltpu.SemaphoreType.DMA((15,)),
            pltpu.SemaphoreType.DMA((copies,)),
            pltpu.SemaphoreType.DMA((copies,)),
        ],
        compiler_params=remote_params(1),
        cost_estimate=cost(50e9, 30 << 20),
        name="middle",
    )(x, ctx, ct, wo, bo, g1, s1, wup, bup, wdn, bdn, g2, s2, lse, mix)


def tail_kernel(
    ndev, parts,
    xp, dq_hbm, dk_hbm, dv_hbm, wq, wk, wv, fg, one_keep, one_got, two_keep, two_got,
    upa_keep, upa_got, upb_keep, upb_got, wo_keep, wo_got, vec, bup,
    ig_ref, dn1_out, dn2_out, up1_out, up2_out, wo_out, q_out, k_out, v_out, vec_out, bup_out,
    one_s, one_r, two_s, two_r, grads, vec_s, vec_r, bup_s, bup_r,
    load_sems, send_sems, recv_sems, upa_s, upb_s, wo_s, qkv_s, *recvs,
):
    rows, width = xp.shape
    loads = []
    for n, src in enumerate((dq_hbm, dk_hbm, dv_hbm)):
        to = grads.at[:, pl.ds(n * width, width)]
        loads.append(pltpu.make_async_copy(src, to, load_sems.at[n]))
    for load in loads:
        load.start()
    links = Links(ndev, parts, send_sems, recv_sems)
    flips = [1 << n for n in range(ndev.bit_length() - 1)]
    links.greet(flips + [(links.shift << 3, links.shift << 4)], False)
    one = Chain(links, one_s, one_r, DN_ONE, 3)
    two = Chain(links, two_s, two_r, DN_TWO, 2)
    recvs = iter(recvs)
    half = 3 * width // 2

    def chain(n, buf, cols=None):
        _, bits, order, step, _, _ = FLATS[n]
        return Flat(links, buf, [next(recvs) for _ in order[step:]], bits, order, step, cols)

    upa, upb, out = (chain(n, buf) for n, buf in enumerate((upa_s, upb_s, wo_s)))
    left = chain(3, qkv_s, slice(0, half))
    right = chain(4, qkv_s, slice(half, 2 * half))

    def begin(chain, keep, got):
        @pl.loop(0, keep.shape[0])
        def _(i):
            chain.buf[i] = both(keep[i], got[i])

        chain.send()

    def begin_flat(chain, keep, got):
        leads = [()]
        for size in keep.shape[:-2]:
            leads = [a + (b,) for a in leads for b in range(size)]

        @pl.loop(0, keep.shape[-2] // 16)
        def _(i):
            at = pl.ds(pl.multiple_of(i * 16, 16), 16)
            for lead in leads:
                index = lead + (at, slice(None))
                chain.buf[index] = both(keep[index], got[index])

        chain.send()

    begin(two, two_keep, two_got)
    begin_flat(upa, upa_keep, upa_got)
    for load in loads:
        load.wait()
    tile = width // 2

    def weights(chain, first_tile):
        @pl.loop(first_tile, first_tile + 3)
        def _(n):
            cols = pl.ds(pl.multiple_of(n * tile, tile), tile)
            part = tn(xp[...], grads[:, cols])
            qkv_s[:, :, :, :, cols] = part.astype(BF16).reshape(2, 2, 2, width // 8, tile)

        chain.send()

    weights(left, 0)
    weights(right, 3)
    begin_flat(upb, upb_keep, upb_got)
    begin_flat(out, wo_keep, wo_got)
    begin(one, one_keep, one_got)
    vec_s[0] = vec[...]
    vec_s[0, 6:7, :] = colsum(grads[:, 0:width].astype(F32))
    vec_s[0, 7:8, :] = colsum(grads[:, 2 * width : 3 * width].astype(F32))
    bup_s[0] = bup[...]

    def vectors(n):
        if n >= len(flips):
            return None
        return [
            links.exchange(vec_s.at[n], vec_r.at[n], flips[n]),
            links.exchange(bup_s.at[n], bup_r.at[n], flips[n]),
        ]

    def add_vectors(n, copies):
        for c in copies:
            c.wait_recv()
        vec_s[n + 1] = vec_s[n] + vec_r[n]
        bup_s[n + 1] = bup_s[n] + bup_r[n]
        return vectors(n + 1)

    pending = vectors(0)
    left.add()
    right.add()

    @pl.loop(0, 2)
    def _(r):
        at = pl.ds(pl.multiple_of(r * (rows // 2), rows // 2), rows // 2)
        total = nt(grads[at, 0:width], wq[...]) + nt(grads[at, width : 2 * width], wk[...])
        total = total + nt(grads[at, 2 * width : 3 * width], wv[...])
        ig_ref[at, :] = (total + fg[at, :]).astype(BF16)

    pending = add_vectors(0, pending)
    two.add()
    upa.add()
    upb.add()
    out.add()
    one.add()
    pending = add_vectors(1, pending)
    left.add()
    right.add()
    pending = add_vectors(2, pending)
    two.add()
    upa.add()
    upb.add()
    out.add()
    one.add()
    left.add()
    right.add()
    pending = add_vectors(3, pending)
    two.add()
    upa.add()
    upb.add()
    out.add()
    dn1_out[...] = one.last()
    dn2_out[...] = two.last()
    up1_out[...] = upa.last()
    up2_out[...] = upb.last()
    wo_out[...] = out.last()
    for n in range(4, len(flips)):
        pending = add_vectors(n, pending)
    vec_out[...] = vec_s[len(flips)]
    bup_out[...] = bup_s[len(flips)]
    left.add()
    right.add()
    mine = left.last()
    q_out[...] = mine[:, 0:width]
    k_out[:, 0:tile] = mine[:, width:]
    mine = right.last()
    k_out[:, tile:] = mine[:, 0:tile]
    v_out[...] = mine[:, tile:]
    links.finish()


FLATS = (
    ("upa", (1,), UP_ONE, 2, 4, 1),
    ("upb", (2, 1), UP_TWO, 2, 4, 2),
    ("out", (1,), OUT_ORDER, 2, 2, 1),
    ("left", (0, 2, 1), LEFT_ORDER, 0, 3, 1),
    ("right", (0, 2, 1), RIGHT_ORDER, 0, 3, 1),
)


def tail(ndev, parts, xp, dq, dk, dv, wq, wk, wv, fg, one, two, upa, upb, wo, vec, bup):
    rows, width = xp.shape
    short = width // BLOCKS
    tall, ff = one[0].shape[1] * 2, upa[0].shape[2] * 2
    steps = ndev.bit_length() - 1

    def out(*shape):
        return jax.ShapeDtypeStruct(shape, F32)

    def chain(step, *shape):
        return [pltpu.VMEM((BLOCKS >> step,) + shape, BF16)] * 2

    flat, received = [], []
    for _, bits, order, step, wide, cut in FLATS:
        cols, tops = wide * width // 2, width // 8 // cut
        flat.append(pltpu.VMEM((2,) * len(bits) + (tops, cols), BF16))
        received += [pltpu.VMEM(u, BF16) for u in flat_recvs(bits, order, step, cols, tops)]
    flat = flat[:3] + [pltpu.VMEM((2, 2, 2, width // 8, 3 * width), BF16)]
    copies = 2 + 3 + 3 * 3 + 2 * 6 + 2 * steps
    return pl.pallas_call(
        functools.partial(tail_kernel, ndev, parts),
        in_specs=[whole()] + [hbm()] * 3 + [whole()] * 16,
        out_specs=[whole()] * 11,
        out_shape=[
            jax.ShapeDtypeStruct((rows, width), BF16),
            out(tall // 2, width), out(tall // 2, width), out(short, ff // 2), out(short, ff // 2),
            out(short, width), out(short, width), out(short, width), out(short, width),
            out(8, width), out(1, ff),
        ],
        scratch_shapes=chain(3, tall // 2, width)
        + chain(2, tall // 2, width)
        + [
            pltpu.VMEM((rows, 3 * width), BF16),
            pltpu.VMEM((steps + 1, 8, width), F32),
            pltpu.VMEM((steps, 8, width), F32),
            pltpu.VMEM((steps + 1, 1, ff), F32),
            pltpu.VMEM((steps, 1, ff), F32),
            pltpu.SemaphoreType.DMA((3,)),
            pltpu.SemaphoreType.DMA((copies,)),
            pltpu.SemaphoreType.DMA((copies,)),
        ] + flat + received,
        compiler_params=remote_params(2),
        cost_estimate=cost(40e9, 16 << 20),
        name="tail",
    )(xp, dq, dk, dv, wq, wk, wv, fg, *one, *two, *upa, *upb, *wo, vec, bup)


def write_kernel(
    ndev, parts, ig, dn1, dn2, up1, up2, wo, q, k, v, vec, bup,
    ig_out, dn_out, up_out, wo_out, q_out, k_out, v_out,
    g2_out, s2_out, db_out, g1_out, s1_out, ob_out, qb_out, vb_out, ub_out,
):
    ig_out[...] = ig[...]
    me = lax.axis_index("dp") * parts + lax.axis_index("seq")
    half = dn1.shape[0]
    dn_out[0:half, :] = dn1[...]
    dn_out[half : 2 * half, :] = dn2[...]
    half = up1.shape[1]
    up_out[:, 0:half] = up1[...]
    up_out[:, half : 2 * half] = up2[...]
    wo_out[...] = wo[...]
    q_out[...] = q[...]
    k_out[...] = k[...]
    v_out[...] = v[...]
    width, ff = vec.shape[1], bup.shape[1]
    mine = width // ndev
    mid = pltpu.roll(vec[...], lax.rem(width - me * mine, width), 1)[:, :128]
    for n, ref in enumerate((g2_out, s2_out, db_out, g1_out, s1_out, ob_out, qb_out, vb_out)):
        ref[...] = mid[n, :mine]
    wide = jnp.broadcast_to(bup[...], (8, ff))
    wide = pltpu.roll(wide, lax.rem(ff - me * (ff // ndev), ff), 1)[:, :128]
    ub_out[...] = wide[0, : ff // ndev]


def write(ndev, parts, ig, dn1, dn2, up1, up2, wo, q, k, v, vec, bup):
    width, ff = vec.shape[1], bup.shape[1]

    def out(*shape):
        return jax.ShapeDtypeStruct(shape, F32)

    shapes = [
        jax.ShapeDtypeStruct(ig.shape, BF16),
        out(2 * dn1.shape[0], width), out(up1.shape[0], ff), out(*wo.shape), out(*q.shape),
        out(*k.shape), out(*v.shape),
    ] + [out(width // ndev)] * 8 + [out(ff // ndev)]
    return pl.pallas_call(
        functools.partial(write_kernel, ndev, parts),
        in_specs=[whole()] * 11,
        out_specs=[whole()] * 16,
        out_shape=shapes,
        compiler_params=params(),
        name="write",
    )(ig, dn1, dn2, up1, up2, wo, q, k, v, vec, bup)


def finish(block, ndev):
    rest = ndev >> LEVELS
    if rest == 1:
        return block
    step = 1
    me = lax.axis_index("dp") * lax.axis_size("seq") + lax.axis_index("seq")
    arr = block.reshape(rest, block.shape[0] // rest, block.shape[1])
    flip = rest
    while flip > 1:
        flip //= 2
        bit = (me // flip) % 2
        half = arr.shape[0] // 2
        keep = lax.dynamic_slice_in_dim(arr, bit * half, half, 0)
        send = lax.dynamic_slice_in_dim(arr, (1 - bit) * half, half, 0)
        arr = keep + lax.ppermute(send, AXES, [(i, i ^ flip) for i in range(ndev)])
    return arr[0]


def shards(
    layer_input,
    query_weight,
    query_bias,
    key_weight,
    value_weight,
    value_bias,
    output_weight,
    output_bias,
    first_gain,
    first_shift,
    up_weight,
    up_bias,
    down_weight,
    down_bias,
    second_gain,
    second_shift,
    out_cotangent,
    passage_lengths,
):
    parts = lax.axis_size("seq")
    ndev = parts * lax.axis_size("dp")
    shift = ndev >> LEVELS
    q, k, v, onehot, qmask, bounds, mix, xp = first(
        ndev, parts, layer_input, passage_lengths, query_weight, query_bias, key_weight,
        value_weight, value_bias,
    )
    ctx, lse = attend_forward(bounds, q, k, v, onehot, qmask)
    (
        result, fg, grads, stat, vec, bup, one_keep, one_send, two_keep, two_send, upa_keep,
        upa_send, upb_keep, upb_send, wo_keep, wo_send,
    ) = middle(
        ndev, parts, layer_input, ctx, out_cotangent, output_weight, output_bias, first_gain,
        first_shift, up_weight, up_bias, down_weight, down_bias, second_gain, second_shift, lse, mix,
    )

    def swap(send, bit):
        flip = shift << bit
        return lax.ppermute(send, AXES, [(i, i ^ flip) for i in range(ndev)])

    two = (two_keep, swap(two_send, DN_TWO[1]))
    upa = (upa_keep, swap(upa_send, UP_ONE[1]))
    upb = (upb_keep, swap(upb_send, UP_TWO[1]))
    one = (one_keep, swap(one_send, DN_ONE[2]))
    wo = (wo_keep, swap(wo_send, OUT_ORDER[1]))
    dq, dk, dv = attend_backward(bounds, q, k, v, grads, stat, onehot, qmask)
    sums = tail(
        ndev, parts, xp, dq, dk, dv, query_weight, key_weight, value_weight, fg, one, two, upa,
        upb, wo, vec, bup,
    )
    ig, dn, up, wo, qg, kg, vg, g2g, s2g, db, g1g, s1g, ob, qb, vb, ub = write(ndev, parts, *sums)
    dn, up, wo, qg, kg, vg = (finish(u, ndev) for u in (dn, up, wo, qg, kg, vg))
    return (
        result, ig, qg, qb, kg, vg, vb, wo, ob, g1g, s1g, up, ub, dn, db, g2g, s2g,
    )


def solution(mesh):
    split = P(AXES, None)
    part = P(AXES)
    in_specs = (split,) + (P(),) * 15 + (split, P("dp", None))
    out_specs = (
        split, split, split, part, split, split, part, split, part, part, part,
        split, part, split, part, part, part,
    )
    return jax.shard_map(shards, mesh=mesh, in_specs=in_specs, out_specs=out_specs, check_vma=False)
```

profile of v0, /device:TPU:0, one launch (start us, length us, event | category | flops | bytes accessed | tf_op | source)
XLA Modules:
  0.0 177.9 jit_solution(11965023932807342704)
XLA Ops:
  0.7 14.1 %first.1 = (bf16[1536,768]{1,0:T(8,128)(2,1)}, bf16[1536,768]{1,0:T(8,128)(2,1)}, bf16[1536,768]{1,0:T(8,128)(2,1)}, bf16[1536,128]{1,0:T(8,128)(2,1)}, bf16[153...) custom-call(bf16[512,768]{1,0:T(8,128)(2,1)} %x_ref.3, ...), custom_call_target="tpu_custom_call" | custom-call | flops 15000000512 | bytes 12582912 | tf_op jit(solution)/shard_map/first/pallas_call | solution.py:443
  14.7 13.7 %attend_forward.1 = (f32[512,768]{1,0:T(8,128)}, f32[6,2,512]{2,1,0:T(2,128)}) custom-call(s32[2,2]{1,0:T(2,128)} %get-tuple-element.73.bounds, bf16[1536,768]{1,0:T(8,128)(2,1)} %get-tuple-element.74.q_ref, bf16[1536,768]{1,0:T(8,128)(2,1)} %get-tuple-element.75.k_ref, bf16[1536,768]{1,0:T(8,128)(2,1)} %get-tuple-element.76.v_ref, ...), custom_call_target="tpu_custom_call" | custom-call | flops 20000000000 | bytes 9437184 | tf_op jit(solution)/shard_map/attend_forward/pallas_call | solution.py:537
  28.5 48.8 %middle.1 = (bf16[512,768]{1,0:T(8,128)(2,1)}, f32[512,768]{1,0:T(8,128)}, bf16[1536,768]{1,0:T(8,128)(2,1)}, f32[6,4,1536]{2,1,0:T(4,128)}, f32[8,768]{1,0:T(8,...) custom-call(bf16[512,768]{1,0:T(8,128)(2,1)} %x_ref.3, ...), custom_call_target="tpu_custom_call" | custom-call | flops 49999998976 | bytes 31457280 | tf_op jit(solution)/shard_map/middle/pallas_call | solution.py:941
  77.3 3.7 %collective-permute-start = (bf16[4,48,768]{2,1,0:T(8,128)(2,1)}, bf16[4,48,768]{2,1,0:T(8,128)(2,1)S(1)}, u32[]{:S(2)}, u32[]{:S(2)}) collective-permute-start(bf16[4,48,768]{2,1,0:T(8,128)(2,1)} %get-tuple-element.91), channel_id=1, source_target_pairs={{0,2},{1,3},{2,0},{3,1},{4,6},{5,7},{6,4},{7,5},{8,10},{9,11},{10,... | collective-permute-start | bytes 884744 | tf_op jit(solution)/shard_map/ppermute | solution.py:1288
  81.0 0.2 collective-permute-start.4
  81.2 0.1 collective-permute-start.1
  81.2 1.8 %collective-permute-start.2 = (bf16[2,96,1536]{2,1,0:T(8,128)(2,1)}, bf16[2,96,1536]{2,1,0:T(8,128)(2,1)S(1)}, u32[]{:S(2)}, u32[]{:S(2)}) collective-permute-start(bf16[2,96,1536]{2,1,0:T(8,128)(2,1)} %get-tuple-element.95), channel_id=1, source_target_pairs={{0,4},{1,5},{2,6},{3,7},{4,0},{5,1},{6,2},{7,3},{8,12},{9,13},{10,... | collective-permute-start | bytes 1769480 | tf_op jit(solution)/shard_map/ppermute | solution.py:1288
  83.1 1.9 %collective-permute-start.3 = (bf16[2,2,48,1536]{3,2,1,0:T(8,128)(2,1)}, bf16[2,2,48,1536]{3,2,1,0:T(8,128)(2,1)S(1)}, u32[]{:S(2)}, u32[]{:S(2)}) collective-permute-start(bf16[2,2,48,1536]{3,2,1,0:T(8,128)(2,1)} %get-tuple-element.97), channel_id=1, source_target_pairs={{0,8},{1,9},{2,10},{3,11},{4,12},{5,13},{6,14},{7,15},{8,0},{9,1},... | collective-permute-start | bytes 1769480 | tf_op jit(solution)/shard_map/ppermute | solution.py:1288
  85.0 25.4 %attend_backward.1 = (bf16[512,768]{1,0:T(8,128)(2,1)}, bf16[512,768]{1,0:T(8,128)(2,1)}, bf16[512,768]{1,0:T(8,128)(2,1)}) custom-call(s32[2,2]{1,0:T(2,128)} %get-tuple-element.73.bounds, bf16[1536,768]{1,0:T(8,128)(2,1)} %get-tuple-element.74.q_ref, bf16[1536,768]{1,0:T(8,128)(2,1)} %get-tuple-element.75.k_ref, ...), custom_call_target="tpu_custom_call" | custom-call | flops 40000000000 | bytes 15728640 | tf_op jit(solution)/shard_map/attend_backward/pallas_call | solution.py:627
  110.3 0.0 collective-permute-done.one_got
  110.3 0.0 copy-start.4
  110.4 0.0 collective-permute-done.4.wo_got
  110.4 0.0 copy-start.5
  110.4 0.0 collective-permute-done.1.two_got
  110.4 0.0 collective-permute-done.2.upa_got
  110.4 0.0 collective-permute-done.3.upb_got
  110.4 0.6 copy-done.4
  111.1 0.1 copy-done.5
  111.2 0.2 copy-done.1
  111.4 0.2 copy-done.2
  111.6 0.2 copy-done.3
  111.7 62.5 %tail.1 = (bf16[512,768]{1,0:T(8,128)(2,1)}, f32[48,768]{1,0:T(8,128)}, f32[48,768]{1,0:T(8,128)}, f32[24,1536]{1,0:T(8,128)}, f32[24,1536]{1,0:T(8,128)}, /*ind...) custom-call(bf16[512,768]{1,0:T(8,128)(2,1)} %get-tuple-element.83.x, ...), custom_call_target="tpu_custom_call" | custom-call | flops 40000000000 | bytes 16777216 | tf_op jit(solution)/shard_map/tail/pallas_call | solution.py:1156
  174.2 2.8 %write.1 = (bf16[512,768]{1,0:T(8,128)(2,1)}, f32[96,768]{1,0:T(8,128)}, f32[24,3072]{1,0:T(8,128)}, f32[24,768]{1,0:T(8,128)}, f32[24,768]{1,0:T(8,128)}, /*ind...) custom-call(bf16[512,768]{1,0:T(8,128)(2,1)} %get-tuple-element.102., ...), custom_call_target="tpu_custom_call" | custom-call | tf_op jit(solution)/shard_map/write/pallas_call | solution.py:1222
  177.0 0.9 copy.36
  (5 shorter events, 0.0 us)
Async XLA Ops:
  77.3 33.1 %collective-permute-start = (bf16[4,48,768]{2,1,0:T(8,128)(2,1)}, bf16[4,48,768]{2,1,0:T(8,128)(2,1)S(1)}, u32[]{:S(2)}, u32[]{:S(2)}) collective-permute-start(bf16[4,48,768]{2,1,0:T(8,128)(2,1)} %get-tuple-element.91), channel_id=1, source_target_pairs={{0,2},{1,3},{2,0},{3,1},{4,6},{5,7},{6,4},{7,5},{8,10},{9,11},{10,... | collective-permute-start | bytes 884744 | tf_op jit(solution)/shard_map/ppermute | solution.py:1288
  81.0 29.4 %collective-permute-start.4 = (bf16[2,96,768]{2,1,0:T(8,128)(2,1)}, bf16[2,96,768]{2,1,0:T(8,128)(2,1)S(1)}, u32[]{:S(2)}, u32[]{:S(2)}) collective-permute-start(bf16[2,96,768]{2,1,0:T(8,128)(2,1)} %get-tuple-element.99), channel_id=1, source_target_pairs={{0,4},{1,5},{2,6},{3,7},{4,0},{5,1},{6,2},{7,3},{8,12},{9,13},{10,... | collective-permute-start | bytes 884744 | tf_op jit(solution)/shard_map/ppermute | solution.py:1288
  81.2 29.2 %collective-permute-start.1 = (bf16[8,48,768]{2,1,0:T(8,128)(2,1)}, bf16[8,48,768]{2,1,0:T(8,128)(2,1)S(1)}, u32[]{:S(2)}, u32[]{:S(2)}) collective-permute-start(bf16[8,48,768]{2,1,0:T(8,128)(2,1)} %get-tuple-element.93), channel_id=1, source_target_pairs={{0,2},{1,3},{2,0},{3,1},{4,6},{5,7},{6,4},{7,5},{8,10},{9,11},{10,... | collective-permute-start | bytes 1769480 | tf_op jit(solution)/shard_map/ppermute | solution.py:1288
  81.2 29.1 %collective-permute-start.2 = (bf16[2,96,1536]{2,1,0:T(8,128)(2,1)}, bf16[2,96,1536]{2,1,0:T(8,128)(2,1)S(1)}, u32[]{:S(2)}, u32[]{:S(2)}) collective-permute-start(bf16[2,96,1536]{2,1,0:T(8,128)(2,1)} %get-tuple-element.95), channel_id=1, source_target_pairs={{0,4},{1,5},{2,6},{3,7},{4,0},{5,1},{6,2},{7,3},{8,12},{9,13},{10,... | collective-permute-start | bytes 1769480 | tf_op jit(solution)/shard_map/ppermute | solution.py:1288
  83.1 27.3 %collective-permute-start.3 = (bf16[2,2,48,1536]{3,2,1,0:T(8,128)(2,1)}, bf16[2,2,48,1536]{3,2,1,0:T(8,128)(2,1)S(1)}, u32[]{:S(2)}, u32[]{:S(2)}) collective-permute-start(bf16[2,2,48,1536]{3,2,1,0:T(8,128)(2,1)} %get-tuple-element.97), channel_id=1, source_target_pairs={{0,8},{1,9},{2,10},{3,11},{4,12},{5,13},{6,14},{7,15},{8,0},{9,1},... | collective-permute-start | bytes 1769480 | tf_op jit(solution)/shard_map/ppermute | solution.py:1288
  110.3 0.7 copy-start.4
  110.4 0.8 copy-start.5
  110.4 1.0 copy-start.1
  110.4 1.1 copy-start.2
  110.4 1.3 copy-start.3
  174.2 2.8 %copy-start = (bf16[512,768]{1,0:T(8,128)(2,1)S(1)}, bf16[512,768]{1,0:T(8,128)(2,1)}, u32[]{:S(2)}) copy-start(bf16[512,768]{1,0:T(8,128)(2,1)} %get-tuple-element.146) | copy-start | bytes 2359300
where the time goes:
time: 177 us; the launch traced here: 178 us
  Pallas kernels  167 us (94%)
  starting transfers between devices  7.71 us (4%)
  local copies, waits for them, and re-layouts  2.2 us (1%)
    pallas_call x1, Pallas kernels, tail(): pl.pallas_call(functools.partial(tail_kernel, ndev, parts), in_specs=[who...  62.5 us
    pallas_call x1, Pallas kernels, middle(): pl.pallas_call(functools.partial(middle_kernel, ndev, parts), in_specs=[w...  48.8 us
    pallas_call x1, Pallas kernels, attend_backward(): pl.pallas_call(backward_kernel, grid_spec=grid, out_shape=[jax.ShapeDtype...  25.4 us
    pallas_call x1, Pallas kernels, first(): pl.pallas_call(functools.partial(first_kernel, ndev, parts), in_specs=[wh...  14.1 us
    pallas_call x1, Pallas kernels, attend_forward(): pl.pallas_call(forward_kernel, grid_spec=grid, out_shape=[jax.ShapeDtypeS...  13.7 us
    ppermute x5, starting transfers between devices, swap(): return lax.ppermute(send, AXES, [(i, i ^ flip) for i in range(ndev)])  7.71 us
  transfers between devices with their start and end apart: 5, of which 0 were waited for; matrix products, arithmetic and copies ran while one was open for 0% of the time, Pallas kernels for 14%

commit v1 on v0

--- a/solution.py
+++ b/solution.py
@@ -56,9 +56,9 @@
     return ref[...].reshape(1, -1)
 
 
-def remote_params(number):
+def remote_params(number, mib):
     return pltpu.CompilerParams(
-        vmem_limit_bytes=60 << 20, collective_id=number, has_side_effects=True
+        vmem_limit_bytes=mib << 20, collective_id=number, has_side_effects=True
     )
 
 
@@ -464,7 +464,7 @@
             pltpu.SemaphoreType.DMA((4,)),
             pltpu.SemaphoreType.DMA((4,)),
         ],
-        compiler_params=remote_params(0),
+        compiler_params=remote_params(0, 26),
         cost_estimate=cost(15e9, 12 << 20),
         name="first",
     )(x, lengths, wq, bq, wk, wv, bv)
@@ -541,7 +541,7 @@
             jax.ShapeDtypeStruct((rows, width), F32),
             jax.ShapeDtypeStruct((pairs, 2, rows), F32),
         ],
-        compiler_params=params(),
+        compiler_params=params(16 << 20),
         cost_estimate=cost(20e9, 24 * rows * width),
         name="attend_forward",
     )(bounds, q, k, v, onehot, qmask)
@@ -628,7 +628,7 @@
         backward_kernel,
         grid_spec=grid,
         out_shape=[jax.ShapeDtypeStruct((rows, width), BF16)] * 3,
-        compiler_params=params(),
+        compiler_params=params(24 << 20),
         cost_estimate=cost(40e9, 40 * rows * width),
         name="attend_backward",
     )(bounds, q, k, v, g, stat, onehot, qmask)
@@ -974,7 +974,7 @@
             pltpu.SemaphoreType.DMA((copies,)),
             pltpu.SemaphoreType.DMA((copies,)),
         ],
-        compiler_params=remote_params(1),
+        compiler_params=remote_params(1, 60),
         cost_estimate=cost(50e9, 30 << 20),
         name="middle",
     )(x, ctx, ct, wo, bo, g1, s1, wup, bup, wdn, bdn, g2, s2, lse, mix)
@@ -1175,7 +1175,7 @@
             pltpu.SemaphoreType.DMA((copies,)),
             pltpu.SemaphoreType.DMA((copies,)),
         ] + flat + received,
-        compiler_params=remote_params(2),
+        compiler_params=remote_params(2, 40),
         cost_estimate=cost(40e9, 16 << 20),
         name="tail",
     )(xp, dq, dk, dv, wq, wk, wv, fg, *one, *two, *upa, *upb, *wo, vec, bup)
@@ -1224,7 +1224,7 @@
         in_specs=[whole()] * 11,
         out_specs=[whole()] * 16,
         out_shape=shapes,
-        compiler_params=params(),
+        compiler_params=params(16 << 20),
         name="write",
     )(ig, dn1, dn2, up1, up2, wo, q, k, v, vec, bup)
 

time: 177 us -> 184 us (1.040)
  local copies, waits for them, and re-layouts: 2.2 us -> 15.7 us
  Pallas kernels: 167 us -> 159 us
    unnamed x13 -> x55, local copies, waits for them, and re-layouts: 2.2 us -> 15.7 us
    pallas_call x1, Pallas kernels: 62.5 us -> 58 us  [tail(): pl.pallas_call(functools.partial(tail_kernel, ndev, parts), in_specs=[who...]
    pallas_call x1, Pallas kernels: 48.8 us -> 46.6 us  [middle(): pl.pallas_call(functools.partial(middle_kernel, ndev, parts), in_specs=[w...]
  transfers between devices with their start and end apart: 5 -> 5, of which waited for: 0 -> 0; matrix products, arithmetic and copies ran while one was open for 0% -> 0% of each run, Pallas kernels for 14% -> 13%
where the time goes in v1:
time: 184 us
  Pallas kernels  159 us (86%)
  local copies, waits for them, and re-layouts  15.7 us (9%)
  starting transfers between devices  8.33 us (5%)
    pallas_call x1, Pallas kernels, tail(): pl.pallas_call(functools.partial(tail_kernel, ndev, parts), in_specs=[who...  58 us
    pallas_call x1, Pallas kernels, middle(): pl.pallas_call(functools.partial(middle_kernel, ndev, parts), in_specs=[w...  46.6 us
    pallas_call x1, Pallas kernels, attend_backward(): pl.pallas_call(backward_kernel, grid_spec=grid, out_shape=[jax.ShapeDtype...  24.7 us
    unnamed x55, local copies, waits for them, and re-layouts  15.7 us
    pallas_call x1, Pallas kernels, first(): pl.pallas_call(functools.partial(first_kernel, ndev, parts), in_specs=[wh...  14.5 us
    pallas_call x1, Pallas kernels, attend_forward(): pl.pallas_call(forward_kernel, grid_spec=grid, out_shape=[jax.ShapeDtypeS...  13.8 us
    ppermute x5, starting transfers between devices, swap(): return lax.ppermute(send, AXES, [(i, i ^ flip) for i in range(ndev)])  8.33 us
  transfers between devices with their start and end apart: 5, of which 0 were waited for; matrix products, arithmetic and copies ran while one was open for 0% of the time, Pallas kernels for 13%

profile of v1, /device:TPU:0, one launch (start us, length us, event | category | flops | bytes accessed | tf_op | source)
XLA Modules:
  0.0 183.9 jit_solution(16857123094937722649)
XLA Ops:
  0.7 1.3 copy-done
  1.9 1.3 copy-done.2
  3.2 1.3 copy-done.4
  4.5 1.1 copy-done.6
  5.6 0.7 copy-done.7
  6.3 0.7 copy-done.8
  7.0 0.7 copy-done.9
  7.6 14.5 %first.1 = (bf16[1536,768]{1,0:T(8,128)(2,1)S(1)}, bf16[1536,768]{1,0:T(8,128)(2,1)S(1)}, bf16[1536,768]{1,0:T(8,128)(2,1)S(1)}, bf16[1536,128]{1,0:T(8,128)(2,1...) custom-call(bf16[512,768]{1,0:T(8,128)(2,1)S(1)} %copy-done.6, ...), custom_call_target="tpu_custom_call" | custom-call | flops 15000000512 | bytes 12582912 | tf_op jit(solution)/shard_map/first/pallas_call | solution.py:443
  22.1 13.8 %attend_forward.1 = (f32[512,768]{1,0:T(8,128)S(1)}, f32[6,2,512]{2,1,0:T(2,128)S(1)}) custom-call(s32[2,2]{1,0:T(2,128)S(1)} %get-tuple-element.73.bounds, bf16[1536,768]{1,0:T(8,128)(2,1)S(1)} %get-tuple-element.74.q_ref, bf16[1536,768]{1,0:T(8,128)(2,1)S(1)} %get-tuple-element.75.k_ref, bf16[1536,768]{1,0:T(8,128)(2,1)S(1)} %get-tuple-element.76.v_ref, ...), custom_call_target="tpu_custom_call" | custom-call | flops 20000000000 | bytes 9437184 | tf_op jit(solution)/shard_map/attend_forward/pallas_call | solution.py:537
  36.0 1.1 copy-done.15
  37.1 0.6 copy-done.23
  37.7 46.6 %middle.1 = (bf16[512,768]{1,0:T(8,128)(2,1)}, f32[512,768]{1,0:T(8,128)}, bf16[1536,768]{1,0:T(8,128)(2,1)}, f32[6,4,1536]{2,1,0:T(4,128)}, f32[8,768]{1,0:T(8,...) custom-call(bf16[512,768]{1,0:T(8,128)(2,1)} %x_ref.3, ...), custom_call_target="tpu_custom_call" | custom-call | flops 49999998976 | bytes 31457280 | tf_op jit(solution)/shard_map/middle/pallas_call | solution.py:941
  84.3 3.8 %collective-permute-start = (bf16[4,48,768]{2,1,0:T(8,128)(2,1)}, bf16[4,48,768]{2,1,0:T(8,128)(2,1)S(1)}, u32[]{:S(2)}, u32[]{:S(2)}) collective-permute-start(bf16[4,48,768]{2,1,0:T(8,128)(2,1)} %get-tuple-element.91), channel_id=1, source_target_pairs={{0,2},{1,3},{2,0},{3,1},{4,6},{5,7},{6,4},{7,5},{8,10},{9,11},{10,... | collective-permute-start | bytes 884744 | tf_op jit(solution)/shard_map/ppermute | solution.py:1288
  88.4 1.9 %collective-permute-start.2 = (bf16[2,96,1536]{2,1,0:T(8,128)(2,1)}, bf16[2,96,1536]{2,1,0:T(8,128)(2,1)S(1)}, u32[]{:S(2)}, u32[]{:S(2)}) collective-permute-start(bf16[2,96,1536]{2,1,0:T(8,128)(2,1)} %get-tuple-element.95), channel_id=1, source_target_pairs={{0,4},{1,5},{2,6},{3,7},{4,0},{5,1},{6,2},{7,3},{8,12},{9,13},{10,... | collective-permute-start | bytes 1769480 | tf_op jit(solution)/shard_map/ppermute | solution.py:1288
  90.3 2.4 %collective-permute-start.3 = (bf16[2,2,48,1536]{3,2,1,0:T(8,128)(2,1)}, bf16[2,2,48,1536]{3,2,1,0:T(8,128)(2,1)S(1)}, u32[]{:S(2)}, u32[]{:S(2)}) collective-permute-start(bf16[2,2,48,1536]{3,2,1,0:T(8,128)(2,1)} %get-tuple-element.97), channel_id=1, source_target_pairs={{0,8},{1,9},{2,10},{3,11},{4,12},{5,13},{6,14},{7,15},{8,0},{9,1},... | collective-permute-start | bytes 1769480 | tf_op jit(solution)/shard_map/ppermute | solution.py:1288
  92.7 1.7 copy-done.11
  94.4 1.7 copy-done.13
  96.0 1.7 copy-done.16
  97.7 0.9 copy-done.22
  98.7 24.7 %attend_backward.1 = (bf16[512,768]{1,0:T(8,128)(2,1)S(1)}, bf16[512,768]{1,0:T(8,128)(2,1)S(1)}, bf16[512,768]{1,0:T(8,128)(2,1)S(1)}) custom-call(s32[2,2]{1,0:T(2,128)S(1)} %get-tuple-element.73.bounds, bf16[1536,768]{1,0:T(8,128)(2,1)S(1)} %get-tuple-element.74.q_ref, bf16[1536,768]{1,0:T(8,128)(2,1)S(1)} %copy-done.11, ...), custom_call_target="tpu_custom_call" | custom-call | flops 40000000000 | bytes 15728640 | tf_op jit(solution)/shard_map/attend_backward/pallas_call | solution.py:627
  123.5 58.0 %tail.1 = (bf16[512,768]{1,0:T(8,128)(2,1)S(1)}, f32[48,768]{1,0:T(8,128)S(1)}, f32[48,768]{1,0:T(8,128)S(1)}, f32[24,1536]{1,0:T(8,128)S(1)}, f32[24,1536]{1,0:...) custom-call(bf16[512,768]{1,0:T(8,128)(2,1)S(1)} %get-tuple-element., ...), custom_call_target="tpu_custom_call" | custom-call | flops 40000000000 | bytes 16777216 | tf_op jit(solution)/shard_map/tail/pallas_call | solution.py:1156
  181.5 1.3 write.1
  182.8 0.2 copy-done.26
  183.0 0.9 copy.36
  (47 shorter events, 0.3 us)
Async XLA Ops:
  0.7 1.3 copy-start
  1.9 1.3 copy-start.2
  22.1 13.8 %copy-start.10 = (bf16[1536,768]{1,0:T(8,128)(2,1)}, bf16[1536,768]{1,0:T(8,128)(2,1)S(1)}, u32[]{:S(2)}) copy-start(bf16[1536,768]{1,0:T(8,128)(2,1)S(1)} %get-tuple-element.75.k_ref) | copy-start | bytes 7077892
  22.1 13.8 %copy-start.12 = (bf16[1536,768]{1,0:T(8,128)(2,1)}, bf16[1536,768]{1,0:T(8,128)(2,1)S(1)}, u32[]{:S(2)}) copy-start(bf16[1536,768]{1,0:T(8,128)(2,1)S(1)} %get-tuple-element.76.v_ref) | copy-start | bytes 7077892
  22.1 13.8 %copy-start.14 = (bf16[768,768]{1,0:T(8,128)(2,1)}, bf16[768,768]{1,0:T(8,128)(2,1)S(1)}, u32[]{:S(2)}) copy-start(bf16[768,768]{1,0:T(8,128)(2,1)S(1)} %get-tuple-element.81.mix) | copy-start | bytes 3538948
  84.3 39.0 %collective-permute-start = (bf16[4,48,768]{2,1,0:T(8,128)(2,1)}, bf16[4,48,768]{2,1,0:T(8,128)(2,1)S(1)}, u32[]{:S(2)}, u32[]{:S(2)}) collective-permute-start(bf16[4,48,768]{2,1,0:T(8,128)(2,1)} %get-tuple-element.91), channel_id=1, source_target_pairs={{0,2},{1,3},{2,0},{3,1},{4,6},{5,7},{6,4},{7,5},{8,10},{9,11},{10,... | collective-permute-start | bytes 884744 | tf_op jit(solution)/shard_map/ppermute | solution.py:1288
  88.2 35.2 %collective-permute-start.4 = (bf16[2,96,768]{2,1,0:T(8,128)(2,1)}, bf16[2,96,768]{2,1,0:T(8,128)(2,1)S(1)}, u32[]{:S(2)}, u32[]{:S(2)}) collective-permute-start(bf16[2,96,768]{2,1,0:T(8,128)(2,1)} %get-tuple-element.99), channel_id=1, source_target_pairs={{0,4},{1,5},{2,6},{3,7},{4,0},{5,1},{6,2},{7,3},{8,12},{9,13},{10,... | collective-permute-start | bytes 884744 | tf_op jit(solution)/shard_map/ppermute | solution.py:1288
  88.3 35.0 %collective-permute-start.1 = (bf16[8,48,768]{2,1,0:T(8,128)(2,1)}, bf16[8,48,768]{2,1,0:T(8,128)(2,1)S(1)}, u32[]{:S(2)}, u32[]{:S(2)}) collective-permute-start(bf16[8,48,768]{2,1,0:T(8,128)(2,1)} %get-tuple-element.93), channel_id=1, source_target_pairs={{0,2},{1,3},{2,0},{3,1},{4,6},{5,7},{6,4},{7,5},{8,10},{9,11},{10,... | collective-permute-start | bytes 1769480 | tf_op jit(solution)/shard_map/ppermute | solution.py:1288
  88.4 35.0 %collective-permute-start.2 = (bf16[2,96,1536]{2,1,0:T(8,128)(2,1)}, bf16[2,96,1536]{2,1,0:T(8,128)(2,1)S(1)}, u32[]{:S(2)}, u32[]{:S(2)}) collective-permute-start(bf16[2,96,1536]{2,1,0:T(8,128)(2,1)} %get-tuple-element.95), channel_id=1, source_target_pairs={{0,4},{1,5},{2,6},{3,7},{4,0},{5,1},{6,2},{7,3},{8,12},{9,13},{10,... | collective-permute-start | bytes 1769480 | tf_op jit(solution)/shard_map/ppermute | solution.py:1288
  90.3 33.1 %collective-permute-start.3 = (bf16[2,2,48,1536]{3,2,1,0:T(8,128)(2,1)}, bf16[2,2,48,1536]{3,2,1,0:T(8,128)(2,1)S(1)}, u32[]{:S(2)}, u32[]{:S(2)}) collective-permute-start(bf16[2,2,48,1536]{3,2,1,0:T(8,128)(2,1)} %get-tuple-element.97), channel_id=1, source_target_pairs={{0,8},{1,9},{2,10},{3,11},{4,12},{5,13},{6,14},{7,15},{8,0},{9,1},... | collective-permute-start | bytes 1769480 | tf_op jit(solution)/shard_map/ppermute | solution.py:1288
  92.7 1.7 copy-start.11
  94.3 1.7 copy-start.13
  96.0 1.7 copy-start.16
  98.6 24.8 %copy-start.1 = (bf16[768,768]{1,0:T(8,128)(2,1)S(1)}, bf16[768,768]{1,0:T(8,128)(2,1)}, u32[]{:S(2)}) copy-start(bf16[768,768]{1,0:T(8,128)(2,1)} %wq.1) | copy-start | bytes 3538948
  98.6 24.8 %copy-start.3 = (bf16[768,768]{1,0:T(8,128)(2,1)S(1)}, bf16[768,768]{1,0:T(8,128)(2,1)}, u32[]{:S(2)}) copy-start(bf16[768,768]{1,0:T(8,128)(2,1)} %wk.1) | copy-start | bytes 3538948
  98.6 24.8 %copy-start.5 = (bf16[768,768]{1,0:T(8,128)(2,1)S(1)}, bf16[768,768]{1,0:T(8,128)(2,1)}, u32[]{:S(2)}) copy-start(bf16[768,768]{1,0:T(8,128)(2,1)} %wv.1) | copy-start | bytes 3538948
  98.6 24.8 %copy-start.17 = (bf16[8,48,768]{2,1,0:T(8,128)(2,1)S(1)}, bf16[8,48,768]{2,1,0:T(8,128)(2,1)}, u32[]{:S(2)}) copy-start(bf16[8,48,768]{2,1,0:T(8,128)(2,1)} %get-tuple-element.92.two_keep) | copy-start | bytes 1769476
  98.6 24.8 %copy-start.18 = (bf16[2,96,1536]{2,1,0:T(8,128)(2,1)S(1)}, bf16[2,96,1536]{2,1,0:T(8,128)(2,1)}, u32[]{:S(2)}) copy-start(bf16[2,96,1536]{2,1,0:T(8,128)(2,1)} %get-tuple-element.94.upa_keep) | copy-start | bytes 1769476
  98.6 24.8 %copy-start.19 = (bf16[2,2,48,1536]{3,2,1,0:T(8,128)(2,1)S(1)}, bf16[2,2,48,1536]{3,2,1,0:T(8,128)(2,1)}, u32[]{:S(2)}) copy-start(bf16[2,2,48,1536]{3,2,1,0:T(8,128)(2,1)} %get-tuple-element.96.upb_keep) | copy-start | bytes 1769476
  98.6 24.8 %copy-start.20 = (bf16[4,48,768]{2,1,0:T(8,128)(2,1)S(1)}, bf16[4,48,768]{2,1,0:T(8,128)(2,1)}, u32[]{:S(2)}) copy-start(bf16[4,48,768]{2,1,0:T(8,128)(2,1)} %get-tuple-element.90.one_keep) | copy-start | bytes 884740
  98.6 24.8 %copy-start.21 = (bf16[2,96,768]{2,1,0:T(8,128)(2,1)S(1)}, bf16[2,96,768]{2,1,0:T(8,128)(2,1)}, u32[]{:S(2)}) copy-start(bf16[2,96,768]{2,1,0:T(8,128)(2,1)} %get-tuple-element.98.wo_keep) | copy-start | bytes 884740
  98.6 24.8 %copy-start.24 = (f32[8,768]{1,0:T(8,128)S(1)}, f32[8,768]{1,0:T(8,128)}, u32[]{:S(2)}) copy-start(f32[8,768]{1,0:T(8,128)} %get-tuple-element.100.vec) | copy-start | bytes 73732
  98.7 24.8 %copy-start.25 = (f32[1,3072]{1,0:T(1,128)S(1)}, f32[1,3072]{1,0:T(1,128)}, u32[]{:S(2)}) copy-start(f32[1,3072]{1,0:T(1,128)} %get-tuple-element.101.bup) | copy-start | bytes 36868
  181.5 1.5 copy-start.26
  (8 other events, 7.1 us)
